TPU v7x, 32 devices: a whole 2x2x4 slice. The times are simulated.
32 devices in a mesh: fsdp: 16 (over z, y, core), ctx: 2 (over x).
Axes of the slice: x: 2, y: 2, z: 4, core: 2. Of those that a mesh axis runs over, the one named last changes fastest.
Arguments:
- tokens: bfloat16 [4096, 1024], P(('fsdp', 'ctx')), may hold values from -6 to 6
- cotangent: bfloat16 [4096, 1024], P(('fsdp', 'ctx')), may hold values from -6 to 6
- seq_lengths: int32 [16, 4], P('fsdp'), may hold values from 1 to 128, 256 in all within a row
- query_key_value_weight: float32 [1024, 4096], P(('fsdp', 'ctx')), may hold values from -0.1875 to 0.1875
- first_moment_projection: float32 [1024, 4096], P(('fsdp', 'ctx')), may hold values from -12 to 12
- second_moment_projection: float32 [1024, 4096], P(('fsdp', 'ctx')), may hold values from 1 to 100
- w_out: float32 [2048, 1024], P(('fsdp', 'ctx')), may hold values from -0.625 to 0.625
- m_out: float32 [2048, 1024], P(('fsdp', 'ctx')), may hold values from -12 to 12
- v_out: float32 [2048, 1024], P(('fsdp', 'ctx')), may hold values from 1 to 100
- w_gateup: float32 [1024, 6144], P(('fsdp', 'ctx')), may hold values from -0.1875 to 0.1875
- m_gateup: float32 [1024, 6144], P(('fsdp', 'ctx')), may hold values from -12 to 12
- v_gateup: float32 [1024, 6144], P(('fsdp', 'ctx')), may hold values from 1 to 100
- w_down: float32 [3072, 1024], P(('fsdp', 'ctx')), may hold values from -0.109375 to 0.109375
- m_down: float32 [3072, 1024], P(('fsdp', 'ctx')), may hold values from -12 to 12
- v_down: float32 [3072, 1024], P(('fsdp', 'ctx')), may hold values from 1 to 100
- attn_gain: float32 [1024], replicated, may hold values from 0.5 to 1.5
- m_attn_gain: float32 [1024], replicated, may hold values from -120 to 120
- v_attn_gain: float32 [1024], replicated, may hold values from 100 to 10000
- mlp_gain: float32 [1024], replicated, may hold values from 0.5 to 1.5
- m_mlp_gain: float32 [1024], replicated, may hold values from -120 to 120
- v_mlp_gain: float32 [1024], replicated, may hold values from 100 to 10000
- q_gain: float32 [128], replicated, may hold values from 0.5 to 1.5
- m_q_gain: float32 [128], replicated, may hold values from -120 to 120
- v_q_gain: float32 [128], replicated, may hold values from 100 to 10000
- k_gain: float32 [128], replicated, may hold values from 0.5 to 1.5
- m_k_gain: float32 [128], replicated, may hold values from -120 to 120
- v_k_gain: float32 [128], replicated, may hold values from 100 to 10000
Outputs:
- output: bfloat16 [4096, 1024], P(('fsdp', 'ctx'))
- grad_tokens: float32 [4096, 1024], P(('fsdp', 'ctx'))
- grad_qkv: float32 [1024, 4096], P(('fsdp', 'ctx'))
- new_w_qkv: float32 [1024, 4096], P(('fsdp', 'ctx'))
- new_m_qkv: float32 [1024, 4096], P(('fsdp', 'ctx'))
- new_v_qkv: float32 [1024, 4096], P(('fsdp', 'ctx'))
- grad_out: float32 [2048, 1024], P(('fsdp', 'ctx'))
- new_w_out: float32 [2048, 1024], P(('fsdp', 'ctx'))
- new_m_out: float32 [2048, 1024], P(('fsdp', 'ctx'))
- new_v_out: float32 [2048, 1024], P(('fsdp', 'ctx'))
- grad_gateup: float32 [1024, 6144], P(('fsdp', 'ctx'))
- new_w_gateup: float32 [1024, 6144], P(('fsdp', 'ctx'))
- new_m_gateup: float32 [1024, 6144], P(('fsdp', 'ctx'))
- new_v_gateup: float32 [1024, 6144], P(('fsdp', 'ctx'))
- grad_down: float32 [3072, 1024], P(('fsdp', 'ctx'))
- new_w_down: float32 [3072, 1024], P(('fsdp', 'ctx'))
- new_m_down: float32 [3072, 1024], P(('fsdp', 'ctx'))
- new_v_down: float32 [3072, 1024], P(('fsdp', 'ctx'))
- grad_attn_gain: float32 [1024], replicated
- new_attn_gain: float32 [1024], replicated
- new_m_attn_gain: float32 [1024], replicated
- new_v_attn_gain: float32 [1024], replicated
- grad_mlp_gain: float32 [1024], replicated
- new_mlp_gain: float32 [1024], replicated
- new_m_mlp_gain: float32 [1024], replicated
- new_v_mlp_gain: float32 [1024], replicated
- grad_q_gain: float32 [128], replicated
- new_q_gain: float32 [128], replicated
- new_m_q_gain: float32 [128], replicated
- new_v_q_gain: float32 [128], replicated
- grad_k_gain: float32 [128], replicated
- new_k_gain: float32 [128], replicated
- new_m_k_gain: float32 [128], replicated
- new_v_k_gain: float32 [128], replicated
Inputs may be any that keep to these rules, and one draw needn't show every extreme that they name: `seq_lengths`: each row holds the lengths of the 4 sequences packed one after another into a group; a row sums to 256 and its largest entry is exactly 128.
All inputs are finite; a program needn't handle non-finite values.
Results may differ from a plain program's by a relative error of at most 0.025.
Values may be sent and summed in bfloat16 or wider, within the bound.
No kernel may reach another device: no remote copies, remote signals or barrier semaphores. Data moves between devices by JAX's collectives and lax.ppermute only.
A program may use at most 256 MiB of HBM per device.

v0:
```python
import math
import jax
import jax.numpy as jnp
from jax import lax
from jax.sharding import PartitionSpec as P

QUERY_HEADS = 16
KEY_VALUE_HEADS = 8
HEAD_WIDTH = 128
FF = 3072
STEP = 3
NORM_EPS = 1e-06
ROPE_BASE = 1000000.0
NEG_LARGE = -1e30
BETA_ONE = 0.9
BETA_TWO = 0.95
ADAM_EPS = 1e-08
MATRIX_RATE = 0.04
GAIN_RATE = 0.2
MATRIX_DECAY = 0.1


def seq_place(lengths, positions):
    ends = jnp.cumsum(lengths)
    passed = ends[None, :] <= positions[:, None]
    segment = jnp.sum(passed.astype(jnp.int32), axis=1)
    start = jnp.sum(jnp.where(passed, lengths[None, :], 0), axis=1)
    return (segment, positions - start)


def rope_tables(offsets, head_size):
    half_size = head_size // 2
    freqs = ROPE_BASE ** (-(2.0 * jnp.arange(half_size, dtype=jnp.float32)) / head_size)
    angles = offsets.astype(jnp.float32)[:, None] * freqs[None, :]
    cosine = jnp.concatenate([jnp.cos(angles), jnp.cos(angles)], axis=1)[:, None, :]
    sine = jnp.concatenate([jnp.sin(angles), jnp.sin(angles)], axis=1)[:, None, :]
    return (cosine, sine)


def rope_apply(values, cosine, sine):
    half_size = values.shape[-1] // 2
    rotated = jnp.concatenate([-values[..., half_size:], values[..., :half_size]], axis=-1)
    return values * cosine + rotated * sine


def rope_back(grads, cosine, sine):
    half_size = grads.shape[-1] // 2
    scaled = grads * sine
    return grads * cosine + jnp.concatenate(
        [scaled[..., half_size:], -scaled[..., :half_size]], axis=-1
    )


def norm_back(grads, values, inv_rms, gain):
    scaled = grads * gain
    return inv_rms * scaled - values * (inv_rms * inv_rms * inv_rms) * jnp.mean(
        scaled * values, axis=-1, keepdims=True
    )


def adamw(weight, first, second, grads, rate, decay):
    new_first = BETA_ONE * first + (1.0 - BETA_ONE) * grads
    new_second = BETA_TWO * second + (1.0 - BETA_TWO) * grads * grads
    first_hat = new_first / (1.0 - BETA_ONE**STEP)
    second_hat = new_second / (1.0 - BETA_TWO**STEP)
    new_weight = weight - rate * (first_hat / (jnp.sqrt(second_hat) + ADAM_EPS) + decay * weight)
    return (new_weight, new_first, new_second)


def reduce_mlp(grad_gateup, grad_down):
    return (
        lax.psum_scatter(grad_gateup, ("fsdp", "ctx"), scatter_dimension=0, tiled=True),
        lax.psum_scatter(grad_down, ("fsdp", "ctx"), scatter_dimension=0, tiled=True),
    )


def reduce_attn(grad_qkv, grad_out):
    return (
        lax.psum_scatter(grad_qkv, ("fsdp", "ctx"), scatter_dimension=0, tiled=True),
        lax.psum_scatter(grad_out, ("fsdp", "ctx"), scatter_dimension=0, tiled=True),
    )


def local(
    tokens,
    cotangent,
    seq_lengths,
    query_key_value_weight,
    first_moment_projection,
    second_moment_projection,
    w_out,
    m_out,
    v_out,
    w_gateup,
    m_gateup,
    v_gateup,
    w_down,
    m_down,
    v_down,
    attn_gain,
    m_attn_gain,
    v_attn_gain,
    mlp_gain,
    m_mlp_gain,
    v_mlp_gain,
    q_gain,
    m_q_gain,
    v_q_gain,
    k_gain,
    m_k_gain,
    v_k_gain,
):
    token_rows = tokens.shape[0]
    ctx_index = lax.axis_index("ctx")
    ctx_count = lax.axis_size("ctx")
    reach_back = ctx_count // 2
    rows_in_window = (reach_back + 1) * token_rows
    heads_per_group = QUERY_HEADS // KEY_VALUE_HEADS
    key_value_width = KEY_VALUE_HEADS * HEAD_WIDTH
    score_scale = 1.0 / math.sqrt(HEAD_WIDTH)
    lengths = seq_lengths[0]
    q_places = ctx_index * token_rows + jnp.arange(token_rows, dtype=jnp.int32)
    q_segment, q_offset = seq_place(lengths, q_places)
    k_places = (ctx_index - reach_back) * token_rows + jnp.arange(rows_in_window, dtype=jnp.int32)
    k_segment, k_unused = seq_place(lengths, k_places)
    k_segment = jnp.where(k_places >= 0, k_segment, -1)
    allowed = (q_segment[:, None] == k_segment[None, :]) & (k_places[None, :] <= q_places[:, None])
    cosine, sine = rope_tables(q_offset, HEAD_WIDTH)
    attn_w, out_w = (
        lax.all_gather(
            query_key_value_weight.astype(jnp.bfloat16), ("fsdp", "ctx"), axis=0, tiled=True
        ),
        lax.all_gather(w_out.astype(jnp.bfloat16), ("fsdp", "ctx"), axis=0, tiled=True),
    )
    gateup_w, down_w = (
        lax.all_gather(w_gateup.astype(jnp.bfloat16), ("fsdp", "ctx"), axis=0, tiled=True),
        lax.all_gather(w_down.astype(jnp.bfloat16), ("fsdp", "ctx"), axis=0, tiled=True),
    )
    tok_float = tokens.astype(jnp.float32)
    inv_one = lax.rsqrt(jnp.mean(tok_float * tok_float, axis=1, keepdims=True) + NORM_EPS)
    normed_one = (tok_float * inv_one * attn_gain).astype(jnp.bfloat16)
    projected_rows = jnp.dot(normed_one, attn_w, preferred_element_type=jnp.float32)
    query = projected_rows[:, : QUERY_HEADS * HEAD_WIDTH].reshape(
        token_rows, QUERY_HEADS, HEAD_WIDTH
    )
    unrotated_key = projected_rows[
        :, QUERY_HEADS * HEAD_WIDTH : QUERY_HEADS * HEAD_WIDTH + key_value_width
    ].reshape(token_rows, KEY_VALUE_HEADS, HEAD_WIDTH)
    unprojected_value = projected_rows[:, QUERY_HEADS * HEAD_WIDTH + key_value_width :]
    inv_q = lax.rsqrt(jnp.mean(query * query, axis=2, keepdims=True) + NORM_EPS)
    inv_k = lax.rsqrt(jnp.mean(unrotated_key * unrotated_key, axis=2, keepdims=True) + NORM_EPS)
    rotated_query = rope_apply(query * inv_q * q_gain, cosine, sine).astype(jnp.bfloat16)
    k_rot = rope_apply(unrotated_key * inv_k * k_gain, cosine, sine).astype(jnp.bfloat16)
    kv_own = jnp.concatenate(
        [k_rot.reshape(token_rows, key_value_width), unprojected_value.astype(jnp.bfloat16)], axis=1
    )
    kv_group = lax.all_gather(kv_own, "ctx", axis=0, tiled=True)
    padded = jnp.concatenate(
        [jnp.zeros((reach_back * token_rows, 2 * key_value_width), jnp.bfloat16), kv_group], axis=0
    )
    key_value_window = lax.dynamic_slice_in_dim(padded, ctx_index * token_rows, rows_in_window, 0)
    key_window = key_value_window[:, :key_value_width].reshape(
        rows_in_window, KEY_VALUE_HEADS, HEAD_WIDTH
    )
    value_window = key_value_window[:, key_value_width:].reshape(
        rows_in_window, KEY_VALUE_HEADS, HEAD_WIDTH
    )
    query_four_dims = rotated_query.reshape(
        token_rows, KEY_VALUE_HEADS, heads_per_group, HEAD_WIDTH
    )
    scores = (
        jnp.einsum(
            "tkgd,jkd->kgtj", query_four_dims, key_window, preferred_element_type=jnp.float32
        )
        * score_scale
    )
    scores = jnp.where(allowed, scores, NEG_LARGE)
    peak = jnp.max(scores, axis=3, keepdims=True)
    expd = jnp.exp(scores - peak)
    totals = jnp.sum(expd, axis=3, keepdims=True)
    log_total = peak + jnp.log(totals)
    probs_half = jnp.exp(scores - log_total).astype(jnp.bfloat16)
    attn_half = jnp.einsum(
        "kgtj,jkd->tkgd", probs_half, value_window, preferred_element_type=jnp.float32
    )
    attn_half = attn_half.reshape(token_rows, QUERY_HEADS * HEAD_WIDTH).astype(jnp.bfloat16)
    resid = tok_float + jnp.dot(attn_half, out_w, preferred_element_type=jnp.float32)
    inv_two = lax.rsqrt(jnp.mean(resid * resid, axis=1, keepdims=True) + NORM_EPS)
    normed_two = (resid * inv_two * mlp_gain).astype(jnp.bfloat16)
    gate_up = jnp.dot(normed_two, gateup_w, preferred_element_type=jnp.float32)
    gate = gate_up[:, :FF]
    upper = gate_up[:, FF:]
    sigm = jax.nn.sigmoid(gate)
    active = gate * sigm
    hidden = (active * upper).astype(jnp.bfloat16)
    output = (resid + jnp.dot(hidden, down_w, preferred_element_type=jnp.float32)).astype(
        jnp.bfloat16
    )
    gateup_back, down_back = (
        lax.all_gather(w_gateup.astype(jnp.bfloat16), ("fsdp", "ctx"), axis=0, tiled=True),
        lax.all_gather(w_down.astype(jnp.bfloat16), ("fsdp", "ctx"), axis=0, tiled=True),
    )
    grad_down = jnp.dot(hidden.T, cotangent, preferred_element_type=jnp.float32)
    grad_hidden = jnp.dot(cotangent, down_back.T, preferred_element_type=jnp.float32)
    grad_gate = grad_hidden * upper * (sigm * (1.0 + gate * (1.0 - sigm)))
    grad_upper = grad_hidden * active
    grad_gu = jnp.concatenate([grad_gate, grad_upper], axis=1).astype(jnp.bfloat16)
    grad_gateup = jnp.dot(normed_two.T, grad_gu, preferred_element_type=jnp.float32)
    share_gateup, share_down = reduce_mlp(grad_gateup, grad_down)
    grad_n_two = jnp.dot(grad_gu, gateup_back.T, preferred_element_type=jnp.float32)
    gain_two = jnp.sum(grad_n_two * resid * inv_two, axis=0)
    grad_resid = cotangent.astype(jnp.float32) + norm_back(grad_n_two, resid, inv_two, mlp_gain)
    resid_half = grad_resid.astype(jnp.bfloat16)
    attn_back, out_back = (
        lax.all_gather(
            query_key_value_weight.astype(jnp.bfloat16), ("fsdp", "ctx"), axis=0, tiled=True
        ),
        lax.all_gather(w_out.astype(jnp.bfloat16), ("fsdp", "ctx"), axis=0, tiled=True),
    )
    grad_out = jnp.dot(attn_half.T, resid_half, preferred_element_type=jnp.float32)
    attention_gradient = jnp.dot(resid_half, out_back.T, preferred_element_type=jnp.float32).astype(
        jnp.bfloat16
    )
    attention_gradient = attention_gradient.reshape(
        token_rows, KEY_VALUE_HEADS, heads_per_group, HEAD_WIDTH
    )
    grad_probs = jnp.einsum(
        "tkgd,jkd->kgtj", attention_gradient, value_window, preferred_element_type=jnp.float32
    )
    probs_full = jnp.exp(scores - log_total)
    grad_scores = probs_full * (
        grad_probs - jnp.sum(probs_full * grad_probs, axis=3, keepdims=True)
    )
    scores_half = (grad_scores * score_scale).astype(jnp.bfloat16)
    grad_qrot = jnp.einsum(
        "kgtj,jkd->tkgd", scores_half, key_window, preferred_element_type=jnp.float32
    ).reshape(token_rows, QUERY_HEADS, HEAD_WIDTH)
    grad_kwin = jnp.einsum(
        "kgtj,tkgd->jkd", scores_half, query_four_dims, preferred_element_type=jnp.float32
    ).reshape(rows_in_window, key_value_width)
    grad_vwin = jnp.einsum(
        "kgtj,tkgd->jkd", probs_half, attention_gradient, preferred_element_type=jnp.float32
    ).reshape(rows_in_window, key_value_width)
    grad_window = jnp.concatenate([grad_kwin, grad_vwin], axis=1)
    placed = jnp.zeros(((reach_back + ctx_count) * token_rows, 2 * key_value_width), jnp.float32)
    placed = lax.dynamic_update_slice_in_dim(placed, grad_window, ctx_index * token_rows, 0)
    local_gradient = lax.psum_scatter(
        placed[reach_back * token_rows :].astype(jnp.bfloat16),
        "ctx",
        scatter_dimension=0,
        tiled=True,
    ).astype(jnp.float32)
    rotated_key_gradient = local_gradient[:, :key_value_width].reshape(
        token_rows, KEY_VALUE_HEADS, HEAD_WIDTH
    )
    grad_value = local_gradient[:, key_value_width:]
    grad_qn = rope_back(grad_qrot, cosine, sine)
    grad_kn = rope_back(rotated_key_gradient, cosine, sine)
    gain_q = jnp.sum(grad_qn * query * inv_q, axis=(0, 1))
    gain_k = jnp.sum(grad_kn * unrotated_key * inv_k, axis=(0, 1))
    grad_query = norm_back(grad_qn, query, inv_q, q_gain).reshape(
        token_rows, QUERY_HEADS * HEAD_WIDTH
    )
    grad_key = norm_back(grad_kn, unrotated_key, inv_k, k_gain).reshape(token_rows, key_value_width)
    grad_proj = jnp.concatenate([grad_query, grad_key, grad_value], axis=1).astype(jnp.bfloat16)
    grad_qkv = jnp.dot(normed_one.T, grad_proj, preferred_element_type=jnp.float32)
    grad_n_one = jnp.dot(grad_proj, attn_back.T, preferred_element_type=jnp.float32)
    gain_one = jnp.sum(grad_n_one * tok_float * inv_one, axis=0)
    grad_tokens = grad_resid + norm_back(grad_n_one, tok_float, inv_one, attn_gain)
    share_qkv, share_out = reduce_attn(grad_qkv, grad_out)
    g_one, g_two, g_q, g_k = lax.psum((gain_one, gain_two, gain_q, gain_k), ("fsdp", "ctx"))
    up_qkv = adamw(
        query_key_value_weight,
        first_moment_projection,
        second_moment_projection,
        share_qkv,
        MATRIX_RATE,
        MATRIX_DECAY,
    )
    up_out = adamw(w_out, m_out, v_out, share_out, MATRIX_RATE, MATRIX_DECAY)
    up_gateup = adamw(w_gateup, m_gateup, v_gateup, share_gateup, MATRIX_RATE, MATRIX_DECAY)
    up_down = adamw(w_down, m_down, v_down, share_down, MATRIX_RATE, MATRIX_DECAY)
    up_one = adamw(attn_gain, m_attn_gain, v_attn_gain, g_one, GAIN_RATE, 0.0)
    up_two = adamw(mlp_gain, m_mlp_gain, v_mlp_gain, g_two, GAIN_RATE, 0.0)
    up_q = adamw(q_gain, m_q_gain, v_q_gain, g_q, GAIN_RATE, 0.0)
    up_k = adamw(k_gain, m_k_gain, v_k_gain, g_k, GAIN_RATE, 0.0)
    return (
        output,
        grad_tokens,
        share_qkv,
        up_qkv[0],
        up_qkv[1],
        up_qkv[2],
        share_out,
        up_out[0],
        up_out[1],
        up_out[2],
        share_gateup,
        up_gateup[0],
        up_gateup[1],
        up_gateup[2],
        share_down,
        up_down[0],
        up_down[1],
        up_down[2],
        g_one,
        up_one[0],
        up_one[1],
        up_one[2],
        g_two,
        up_two[0],
        up_two[1],
        up_two[2],
        g_q,
        up_q[0],
        up_q[1],
        up_q[2],
        g_k,
        up_k[0],
        up_k[1],
        up_k[2],
    )


def solution(mesh):
    in_specs = (
        P(("fsdp", "ctx"), None),
        P(("fsdp", "ctx"), None),
        P("fsdp", None),
        P(("fsdp", "ctx"), None),
        P(("fsdp", "ctx"), None),
        P(("fsdp", "ctx"), None),
        P(("fsdp", "ctx"), None),
        P(("fsdp", "ctx"), None),
        P(("fsdp", "ctx"), None),
        P(("fsdp", "ctx"), None),
        P(("fsdp", "ctx"), None),
        P(("fsdp", "ctx"), None),
        P(("fsdp", "ctx"), None),
        P(("fsdp", "ctx"), None),
        P(("fsdp", "ctx"), None),
        P(),
        P(),
        P(),
        P(),
        P(),
        P(),
        P(),
        P(),
        P(),
        P(),
        P(),
        P(),
    )
    out_specs = (
        P(("fsdp", "ctx"), None),
        P(("fsdp", "ctx"), None),
        P(("fsdp", "ctx"), None),
        P(("fsdp", "ctx"), None),
        P(("fsdp", "ctx"), None),
        P(("fsdp", "ctx"), None),
        P(("fsdp", "ctx"), None),
        P(("fsdp", "ctx"), None),
        P(("fsdp", "ctx"), None),
        P(("fsdp", "ctx"), None),
        P(("fsdp", "ctx"), None),
        P(("fsdp", "ctx"), None),
        P(("fsdp", "ctx"), None),
        P(("fsdp", "ctx"), None),
        P(("fsdp", "ctx"), None),
        P(("fsdp", "ctx"), None),
        P(("fsdp", "ctx"), None),
        P(("fsdp", "ctx"), None),
        P(),
        P(),
        P(),
        P(),
        P(),
        P(),
        P(),
        P(),
        P(),
        P(),
        P(),
        P(),
        P(),
        P(),
        P(),
        P(),
    )
    return jax.shard_map(local, mesh=mesh, in_specs=in_specs, out_specs=out_specs, check_vma=False)
```

profile of v0, /device:TPU:11, one launch (start us, length us, event | category | flops | bytes accessed | tf_op | source)
XLA Modules:
  0.0 1383.0 jit_solution(14045614941543385687)
XLA Ops:
  7.3 1.8 convert_element_type.83
  10.0 1.2 fusion.66
  13.0 1.1 fusion.29
  15.3 74.9 %all-gather.6.cloned.1.call-done = bf16[1024,4096]{1,0:T(8,128)(2,1)} async-done(((bf16[32,4096]{1,0:T(8,128)(2,1)}), bf16[1024,4096]{1,0:T(8,128)(2,1)}) %all-gather.6.cloned.1.call-update) | async-done | bytes 8388624 | tf_op jit(solution)/shard_map/all_gather | solution.py:130
  90.2 4.7 fusion.61
  97.7 1.0 multiply_multiply_fusion.4
  98.9 1.0 maximum_multiply_fusion.1
  101.9 1.7 convert_element_type.93
  103.6 1.9 convert_element_type.95
  106.8 1.4 compare_and_fusion
  110.2 10.2 all-gather.8.cloned.1.call-done
  120.4 1.4 fusion.38
  123.4 0.9 copy-done.1
  124.9 62.0 %all-gather.10.cloned.1.call-done = bf16[2048,1024]{1,0:T(8,128)(2,1)} async-done(((bf16[64,1024]{1,0:T(8,128)(2,1)}), bf16[2048,1024]{1,0:T(8,128)(2,1)}) %all-gather.10.cloned.1.call-update) | async-done | bytes 4194320 | tf_op jit(solution)/shard_map/all_gather | solution.py:133
  186.9 3.0 multiply_reduce_fusion.5
  190.6 93.7 %all-gather.12.cloned.1.call-done = bf16[1024,6144]{1,0:T(8,128)(2,1)} async-done(((bf16[32,6144]{1,0:T(8,128)(2,1)}), bf16[1024,6144]{1,0:T(8,128)(2,1)}) %all-gather.12.cloned.1.call-update) | async-done | bytes 12582928 | tf_op jit(solution)/shard_map/all_gather | solution.py:136
  284.2 8.1 fusion.77
  292.3 63.4 %all-gather.14.cloned.1.call-done = bf16[3072,1024]{1,0:T(8,128)(2,1)} async-done(((bf16[96,1024]{1,0:T(8,128)(2,1)}), bf16[3072,1024]{1,0:T(8,128)(2,1)}) %all-gather.14.cloned.1.call-update) | async-done | bytes 6291472 | tf_op jit(solution)/shard_map/all_gather | solution.py:137
  355.7 7.7 multiply_convert_fusion.1
  363.4 7.2 multiply_reduce_fusion.2
  370.7 1.5 subtract_add_fusion
  372.2 4.6 convolution_convert_fusion
  376.7 2.7 copy.188
  379.4 2.9 fusion.48
  382.4 1.3 fusion.53
  383.7 4.2 fusion.6
  387.9 1.2 copy.186
  389.1 2.0 copy.187
  391.3 1.1 maximum_dynamic-update-slice_fusion
  392.5 1.1 slice.129
  393.7 4.5 fusion.57
  399.2 7.5 fusion.89
  406.8 1.0 copy-done.6
  407.7 11.6 fusion.24
  419.6 1.1 mul.787
  420.7 2.6 copy.151
  423.3 1.3 broadcast_bitcast_fusion
  424.5 1.1 mul.754
  425.6 2.5 copy.153
  428.1 1.4 copy.154
  429.6 1.4 copy.161
  431.0 4.4 fusion.7
  435.3 1.5 bitcast_multiply_fusion.9
  437.7 1.3 copy.152
  439.0 2.8 copy.185
  443.3 3.6 multiply_reduce_fusion
  446.9 1.8 convert_bitcast_fusion
  449.6 1.0 fusion.43
  451.4 1.3 broadcast_multiply_fusion.1
  454.0 2.1 fusion.46
  456.8 8.2 fusion.50
  465.0 1.1 copy-done.22
  466.1 4.6 fusion.9
  470.9 6.5 fusion.37
  477.4 40.1 %all-reduce.1 = (f32[1024]{0:T(1024)S(1)}, f32[1024]{0:T(1024)S(1)}, f32[128]{0:T(128)S(1)}, f32[128]{0:T(128)S(1)}) all-reduce(f32[1024]{0:T(1024)S(1)} %get-tuple-element.36, f32[1024]{0:T(1024)S(1)} %copy-done.58, f32[128]{0:T(128)S(1)} %bitcast_reduce_fusion, ...), channel_id=1, replica_groups=mesh['fsdp'=16,'ctx'=2] {'fsdp','ctx'}, use_global_device_ids=true, to_apply=%region_21.22 | all-reduce | flops 2304 | bytes 18432 | tf_op jit(solution)/shard_map/psum | solution.py:271
  519.9 1.0 fusion.34
  520.9 80.5 %reduce-scatter.10.cloned.1.call-done = f32[64,1024]{1,0:T(8,128)} async-done(((f32[2048,1024]{1,0:T(8,128)}), f32[64,1024]{1,0:T(8,128)}) %reduce-scatter.10.cloned.1.call-update) | async-done | bytes 262160 | tf_op jit(solution)/shard_map/reduce_scatter | solution.py:80
  601.4 2.1 multiply_subtract_fusion.3
  603.5 156.3 %reduce-scatter.14.cloned.1.call-done = f32[96,1024]{1,0:T(8,128)} async-done(((f32[3072,1024]{1,0:T(8,128)}), f32[96,1024]{1,0:T(8,128)}) %reduce-scatter.14.cloned.1.call-update) | async-done | bytes 393232 | tf_op jit(solution)/shard_map/reduce_scatter | solution.py:73
  759.9 2.4 multiply_subtract_fusion.2
  762.3 248.6 %reduce-scatter.12.cloned.1.call-done = f32[32,6144]{1,0:T(8,128)} async-done(((f32[1024,6144]{1,0:T(8,128)}), f32[32,6144]{1,0:T(8,128)}) %reduce-scatter.12.cloned.1.call-update) | async-done | bytes 786448 | tf_op jit(solution)/shard_map/reduce_scatter | solution.py:72
  1010.9 2.9 multiply_subtract_fusion
  1013.8 359.6 %reduce-scatter.8.cloned.1.call-done = f32[32,4096]{1,0:T(8,128)} async-done(((f32[1024,4096]{1,0:T(8,128)}), f32[32,4096]{1,0:T(8,128)}) %reduce-scatter.8.cloned.1.call-update) | async-done | bytes 524304 | tf_op jit(solution)/shard_map/reduce_scatter | solution.py:79
  1373.4 2.6 multiply_subtract_fusion.1
  (244 shorter events, 24.3 us)
Async XLA Ops:
  7.2 83.0 %copy-start.12 = (bf16[128,1024]{1,0:T(8,128)(2,1)S(1)}, bf16[128,1024]{1,0:T(8,128)(2,1)}, u32[]{:S(2)}) copy-start(bf16[128,1024]{1,0:T(8,128)(2,1)} %param.27) | copy-start | bytes 786436
  7.2 83.0 %all-gather.6.cloned.1.call-start = ((), (), s32[]{:S(2)}) async-start(), calls=%async_computation.5 | async-start | bytes 8650752 | tf_op jit(solution)/shard_map/all_gather | solution.py:130
  9.1 111.3 %all-gather.8.cloned.1.call-start = ((), (), s32[]{:S(2)}) async-start(), calls=%async_computation.6 | async-start | bytes 1572864 | tf_op jit(solution)/shard_map/all_gather | solution.py:157
  10.0 80.3 %copy-start.72 = (s32[4,1]{0,1:T(1,128)}, s32[4,1]{0,1:T(1,128)S(1)}, u32[]{:S(2)}) copy-start(s32[4,1]{0,1:T(1,128)S(1)} %reduce-window.8) | copy-start | bytes 52
  14.6 80.3 %copy-start.56 = (f32[128]{0:T(128)}, f32[128]{0:T(128)S(1)}, u32[]{:S(2)}) copy-start(f32[128]{0:T(128)S(1)} %get-tuple-element.98) | copy-start | bytes 1540
  95.0 13.3 copy-start.7
  95.0 2.7 copy-start.62
  96.0 4.0 copy-start.10
  100.3 3.3 copy-start.16
  100.9 5.8 copy-start.73
  101.8 85.1 %all-gather.10.cloned.1.call-start = ((), (), s32[]{:S(2)}) async-start(), calls=%async_computation.7 | async-start | bytes 4325376 | tf_op jit(solution)/shard_map/all_gather | solution.py:133
  101.9 3.8 copy-start.30
  103.6 180.7 %all-gather.12.cloned.1.call-start = ((), (), s32[]{:S(2)}) async-start(), calls=%async_computation.8 | async-start | bytes 12976128 | tf_op jit(solution)/shard_map/all_gather | solution.py:136
  105.6 250.2 %all-gather.14.cloned.1.call-start = ((), (), s32[]{:S(2)}) async-start(), calls=%async_computation.9 | async-start | bytes 6488064 | tf_op jit(solution)/shard_map/all_gather | solution.py:137
  106.4 340.5 %reduce-scatter.6.cloned.1.call-start = ((), (), s32[]{:S(2)}) async-start(), calls=%async_computation.10 | async-start | bytes 1572864 | tf_op jit(solution)/shard_map/reduce_scatter | solution.py:247
  110.2 12.2 copy-start.26
  123.4 66.5 %copy-start.51 = (f32[2,8,128]{2,1,0:T(8,128)}, f32[2,8,128]{2,1,0:T(8,128)S(1)}, u32[]{:S(2)}) copy-start(f32[2,8,128]{2,1,0:T(8,128)S(1)} %log_add_fusion) | copy-start | bytes 24580
  124.9 65.1 %copy-start.13 = (bf16[8,128,2,128]{3,1,2,0:T(8,128)(2,1)}, bf16[8,128,2,128]{3,1,2,0:T(8,128)(2,1)S(1)}, u32[]{:S(2)}) copy-start(bf16[8,128,2,128]{3,1,2,0:T(8,128)(2,1)S(1)} %convolution_convert_fusion.1) | copy-start | bytes 1572868
  186.9 97.3 %copy-start.41 = (f32[1024]{0:T(1024)S(1)}, f32[1024]{0:T(1024)}, u32[]{:S(2)}) copy-start(f32[1024]{0:T(1024)} %param.45) | copy-start | bytes 12292
  190.0 102.3 %copy-start.5 = (f32[128,1024]{1,0:T(8,128)}, f32[128,1024]{1,0:T(8,128)S(1)}, u32[]{:S(2)}) copy-start(f32[128,1024]{1,0:T(8,128)S(1)} %get-tuple-element.104) | copy-start | bytes 1572868
  190.6 172.9 %copy-start.55 = (f32[128]{0:T(128)}, f32[128]{0:T(128)S(1)}, u32[]{:S(2)}) copy-start(f32[128]{0:T(128)S(1)} %get-tuple-element.100) | copy-start | bytes 1540
  355.7 7.7 copy-start
  372.2 7.3 copy-start.18
  376.7 5.7 copy-start.2
  379.4 3.0 copy-start.19
  379.4 3.0 copy-start.52
  393.6 207.8 %reduce-scatter.10.cloned.1.call-start = ((), (), s32[]{:S(2)}) async-start(), calls=%async_computation.12 | async-start | bytes 8650752 | tf_op jit(solution)/shard_map/reduce_scatter | solution.py:80
  398.2 361.7 %reduce-scatter.14.cloned.1.call-start = ((), (), s32[]{:S(2)}) async-start(), calls=%async_computation.14 | async-start | bytes 12976128 | tf_op jit(solution)/shard_map/reduce_scatter | solution.py:73
  406.7 604.2 %reduce-scatter.12.cloned.1.call-start = ((), (), s32[]{:S(2)}) async-start(), calls=%async_computation.13 | async-start | bytes 25952256 | tf_op jit(solution)/shard_map/reduce_scatter | solution.py:72
  419.4 954.0 %reduce-scatter.8.cloned.1.call-start = ((), (), s32[]{:S(2)}) async-start(), calls=%async_computation.11 | async-start | bytes 17301504 | tf_op jit(solution)/shard_map/reduce_scatter | solution.py:79
  425.6 5.4 copy-start.53
  439.0 3.1 copy-start.49
  439.0 3.4 copy-start.8
  449.6 4.1 copy-start.48
  453.7 3.1 copy-start.28
  453.7 3.1 copy-start.34
  453.7 3.0 copy-start.42
  453.8 3.0 copy-start.57
  466.1 4.6 copy-start.29
  466.1 4.6 copy-start.33
  466.1 4.6 copy-start.35
  470.8 6.6 copy-start.58
  470.8 46.7 %copy-start.64 = (f32[128]{0:T(128)S(1)}, f32[128]{0:T(128)}, u32[]{:S(2)}) copy-start(f32[128]{0:T(128)} %param.51) | copy-start | bytes 1540
  470.8 46.7 %copy-start.74 = (f32[128]{0:T(128)S(1)}, f32[128]{0:T(128)}, u32[]{:S(2)}) copy-start(f32[128]{0:T(128)} %param.52) | copy-start | bytes 1540
  470.8 46.7 %copy-start.75 = (f32[128]{0:T(128)S(1)}, f32[128]{0:T(128)}, u32[]{:S(2)}) copy-start(f32[128]{0:T(128)} %param.53) | copy-start | bytes 1540
  470.8 47.3 %copy-start.61 = (f32[128]{0:T(128)S(1)}, f32[128]{0:T(128)}, u32[]{:S(2)}) copy-start(f32[128]{0:T(128)} %param.48) | copy-start | bytes 1540
  470.8 47.3 %copy-start.76 = (f32[128]{0:T(128)S(1)}, f32[128]{0:T(128)}, u32[]{:S(2)}) copy-start(f32[128]{0:T(128)} %param.49) | copy-start | bytes 1540
  470.8 47.3 %copy-start.77 = (f32[128]{0:T(128)S(1)}, f32[128]{0:T(128)}, u32[]{:S(2)}) copy-start(f32[128]{0:T(128)} %param.50) | copy-start | bytes 1540
  470.9 47.8 %copy-start.65 = (f32[1024]{0:T(1024)S(1)}, f32[1024]{0:T(1024)}, u32[]{:S(2)}) copy-start(f32[1024]{0:T(1024)} %param.46) | copy-start | bytes 12292
  470.9 47.8 %copy-start.66 = (f32[1024]{0:T(1024)S(1)}, f32[1024]{0:T(1024)}, u32[]{:S(2)}) copy-start(f32[1024]{0:T(1024)} %param.47) | copy-start | bytes 12292
  470.9 48.4 %copy-start.67 = (f32[1024]{0:T(1024)S(1)}, f32[1024]{0:T(1024)}, u32[]{:S(2)}) copy-start(f32[1024]{0:T(1024)} %param.43) | copy-start | bytes 12292
  470.9 48.4 %copy-start.68 = (f32[1024]{0:T(1024)S(1)}, f32[1024]{0:T(1024)}, u32[]{:S(2)}) copy-start(f32[1024]{0:T(1024)} %param.44) | copy-start | bytes 12292
  470.9 49.0 %copy-start.80 = (f32[128]{0:T(128)S(1)}, f32[128]{0:T(128)}, u32[]{:S(2)}) copy-start(f32[128]{0:T(128)} %get-tuple-element.97) | copy-start | bytes 1540
  477.4 124.1 %copy-start.37 = (f32[64,1024]{1,0:T(8,128)S(1)}, f32[64,1024]{1,0:T(8,128)}, u32[]{:S(2)}) copy-start(f32[64,1024]{1,0:T(8,128)} %param.33) | copy-start | bytes 786436
  477.4 282.5 %copy-start.31 = (f32[96,1024]{1,0:T(8,128)S(1)}, f32[96,1024]{1,0:T(8,128)}, u32[]{:S(2)}) copy-start(f32[96,1024]{1,0:T(8,128)} %param.39) | copy-start | bytes 1179652
  517.5 242.3 %copy-start.79 = (f32[128]{0:T(128)}, f32[128]{0:T(128)S(1)}, u32[]{:S(2)}) copy-start(f32[128]{0:T(128)S(1)} %get-tuple-element.43) | copy-start | bytes 1540
  517.5 244.8 %copy-start.69 = (f32[1024]{0:T(1024)}, f32[1024]{0:T(1024)S(1)}, u32[]{:S(2)}) copy-start(f32[1024]{0:T(1024)S(1)} %get-tuple-element.40) | copy-start | bytes 12292
  517.5 244.8 %copy-start.70 = (f32[1024]{0:T(1024)}, f32[1024]{0:T(1024)S(1)}, u32[]{:S(2)}) copy-start(f32[1024]{0:T(1024)S(1)} %get-tuple-element.41) | copy-start | bytes 12292
  517.5 244.8 %copy-start.78 = (f32[128]{0:T(128)}, f32[128]{0:T(128)S(1)}, u32[]{:S(2)}) copy-start(f32[128]{0:T(128)S(1)} %get-tuple-element.42) | copy-start | bytes 1540
  520.9 490.0 %copy-start.23 = (f32[32,6144]{1,0:T(8,128)S(1)}, f32[32,6144]{1,0:T(8,128)}, u32[]{:S(2)}) copy-start(f32[32,6144]{1,0:T(8,128)} %param.36) | copy-start | bytes 2359300
  520.9 490.0 %copy-start.39 = (f32[32,6144]{1,0:T(8,128)S(1)}, f32[32,6144]{1,0:T(8,128)}, u32[]{:S(2)}) copy-start(f32[32,6144]{1,0:T(8,128)} %param.37) | copy-start | bytes 2359300
  520.9 490.0 %copy-start.40 = (f32[32,6144]{1,0:T(8,128)S(1)}, f32[32,6144]{1,0:T(8,128)}, u32[]{:S(2)}) copy-start(f32[32,6144]{1,0:T(8,128)} %param.38) | copy-start | bytes 2359300
  762.3 611.1 %copy-start.24 = (f32[32,4096]{1,0:T(8,128)S(1)}, f32[32,4096]{1,0:T(8,128)}, u32[]{:S(2)}) copy-start(f32[32,4096]{1,0:T(8,128)} %param.30) | copy-start | bytes 1572868
  762.3 611.1 %copy-start.47 = (f32[32,4096]{1,0:T(8,128)S(1)}, f32[32,4096]{1,0:T(8,128)}, u32[]{:S(2)}) copy-start(f32[32,4096]{1,0:T(8,128)} %param.31) | copy-start | bytes 1572868
  (27 other events, 34.1 us)
Sparse Core Ops, SparseCore 0:
  11.6 78.6 all-gather.5
  101.9 18.4 all-gather.7
  124.0 62.9 all-gather.9
  190.3 93.9 all-gather.11
  287.6 68.1 all-gather.13
  393.7 17.4 reduce-scatter.5
  414.1 187.3 reduce-scatter.9
  608.0 151.7 reduce-scatter.13
  766.9 244.0 reduce-scatter.11
  1013.6 359.7 reduce-scatter.7
where the time goes:
time: 1390 us; the launch traced here: 1380 us
  waiting for transfers between devices  1150 us (83%)
  matrix products  92 us (7%)
  other arithmetic  46.4 us (3%)
  blocking collectives  40.1 us (3%)
  local copies, waits for them, and re-layouts  38.9 us (3%)
  between operations  15.4 us (1%)
    reduce_scatter x1, waiting for transfers between devices, reduce_attn(): lax.psum_scatter(grad_qkv, ('fsdp', 'ctx'), scatter_dimension=0, tiled=True)  360 us
    reduce_scatter x1, waiting for transfers between devices, reduce_mlp(): lax.psum_scatter(grad_gateup, ('fsdp', 'ctx'), scatter_dimension=0, tiled...  249 us
    reduce_scatter x1, waiting for transfers between devices, reduce_mlp(): lax.psum_scatter(grad_down, ('fsdp', 'ctx'), scatter_dimension=0, tiled=T...  156 us
    all_gather x1, waiting for transfers between devices, local(): lax.all_gather(w_gateup.astype(jnp.bfloat16), ('fsdp', 'ctx'), axis=0, ti...  93.7 us
    reduce_scatter x1, waiting for transfers between devices, reduce_attn(): lax.psum_scatter(grad_out, ('fsdp', 'ctx'), scatter_dimension=0, tiled=True)  80.5 us
    all_gather x1, waiting for transfers between devices, local(): lax.all_gather(query_key_value_weight.astype(jnp.bfloat16), ('fsdp', 'ctx...  74.9 us
    all_gather x1, waiting for transfers between devices, local(): lax.all_gather(w_down.astype(jnp.bfloat16), ('fsdp', 'ctx'), axis=0, tile...  63.4 us
    all_gather x1, waiting for transfers between devices, local(): lax.all_gather(w_out.astype(jnp.bfloat16), ('fsdp', 'ctx'), axis=0, tiled...  62 us
  transfers between devices with their start and end apart: 10, of which 9 were waited for; matrix products, arithmetic and copies ran while one was open for 8% of the time, Pallas kernels for 0%

commit v1 on v0

--- a/solution.py
+++ b/solution.py
@@ -3,6 +3,7 @@
 import jax.numpy as jnp
 from jax import lax
 from jax.sharding import PartitionSpec as P
+from jax.lax import axis_index, axis_size, ppermute
 
 QUERY_HEADS = 16
 KEY_VALUE_HEADS = 8
@@ -18,6 +19,28 @@
 MATRIX_RATE = 0.04
 GAIN_RATE = 0.2
 MATRIX_DECAY = 0.1
+
+
+def play_leaf(x_local, at_axis):
+    state_next = list(x_local.shape[1:])
+    state_next[at_axis] *= x_local.shape[0]
+    return jnp.moveaxis(x_local, 0, at_axis).reshape(state_next)
+
+
+def stages_all_touch(t0, a_name):
+    moved = axis_index(a_name)
+    then = axis_size(a_name)
+    main, before = (then, moved)
+    reply, mixed_arr = (t0[None], 1)
+    while mixed_arr < main:
+        w_next = list(map(lambda j: (j, j ^ mixed_arr), range(main)))
+        f_now = ppermute(reply, a_name, w_next)
+        vec_out = before & mixed_arr == 0
+        even = jnp.where(vec_out, reply, f_now)
+        n_now = jnp.where(vec_out, f_now, reply)
+        reply = jnp.concatenate([even, n_now])
+        mixed_arr *= 2
+    return reply
 
 
 def seq_place(lengths, positions):
@@ -110,6 +133,11 @@
     m_k_gain,
     v_k_gain,
 ):
+
+    def recast_forms_over_axis(field_in, x_in, ndim_at):
+        piece_now = stages_all_touch(field_in, x_in)
+        return play_leaf(piece_now, ndim_at)
+
     token_rows = tokens.shape[0]
     ctx_index = lax.axis_index("ctx")
     ctx_count = lax.axis_size("ctx")
@@ -133,7 +161,7 @@
         lax.all_gather(w_out.astype(jnp.bfloat16), ("fsdp", "ctx"), axis=0, tiled=True),
     )
     gateup_w, down_w = (
-        lax.all_gather(w_gateup.astype(jnp.bfloat16), ("fsdp", "ctx"), axis=0, tiled=True),
+        recast_forms_over_axis(w_gateup.astype(jnp.bfloat16), ("fsdp", "ctx"), 0),
         lax.all_gather(w_down.astype(jnp.bfloat16), ("fsdp", "ctx"), axis=0, tiled=True),
     )
     tok_float = tokens.astype(jnp.float32)

time: 1390 us -> 1660 us (1.19)
  waiting for transfers between devices: 1150 us -> 1380 us
  other arithmetic: 46.4 us -> 63.9 us
    ppermute x0 -> x5, waiting for transfers between devices: none -> 430 us  [stages_all_touch(): f_now = ppermute(reply, a_name, w_next)]
    reduce_scatter x1, waiting for transfers between devices: 156 us -> 49.3 us  [reduce_mlp(): lax.psum_scatter(grad_down, ('fsdp', 'ctx'), scatter_dimension=0, tiled=T...]
    reduce_scatter x1, waiting for transfers between devices: 80.5 us -> 187 us  [reduce_attn(): lax.psum_scatter(grad_out, ('fsdp', 'ctx'), scatter_dimension=0, tiled=True)]
    all_gather x1, waiting for transfers between devices: 63.4 us -> 0.01 us  [local(): lax.all_gather(w_down.astype(jnp.bfloat16), ('fsdp', 'ctx'), axis=0, tile...]
    all_gather x1, waiting for transfers between devices: 62 us -> 0.01 us  [local(): lax.all_gather(w_out.astype(jnp.bfloat16), ('fsdp', 'ctx'), axis=0, tiled...]
    all_gather x1, waiting for transfers between devices: 93.7 us -> 33 us  [local(): lax.all_gather(w_gateup.astype(jnp.bfloat16), ('fsdp', 'ctx'), axis=0, ti...]
  transfers between devices with their start and end apart: 10 -> 15, of which waited for: 9 -> 11; matrix products, arithmetic and copies ran while one was open for 8% -> 9% of each run, Pallas kernels for 0% -> 0%
where the time goes in v1:
time: 1660 us; the launch traced here: 1650 us
  waiting for transfers between devices  1380 us (83%)
  matrix products  101 us (6%)
  other arithmetic  63.9 us (4%)
  blocking collectives  41.8 us (3%)
  local copies, waits for them, and re-layouts  41.2 us (2%)
    ppermute x5, waiting for transfers between devices, stages_all_touch(): f_now = ppermute(reply, a_name, w_next)  430 us
    reduce_scatter x1, waiting for transfers between devices, reduce_attn(): lax.psum_scatter(grad_qkv, ('fsdp', 'ctx'), scatter_dimension=0, tiled=True)  360 us
    reduce_scatter x1, waiting for transfers between devices, reduce_mlp(): lax.psum_scatter(grad_gateup, ('fsdp', 'ctx'), scatter_dimension=0, tiled...  247 us
    reduce_scatter x1, waiting for transfers between devices, reduce_attn(): lax.psum_scatter(grad_out, ('fsdp', 'ctx'), scatter_dimension=0, tiled=True)  187 us
    all_gather x1, waiting for transfers between devices, local(): lax.all_gather(query_key_value_weight.astype(jnp.bfloat16), ('fsdp', 'ctx...  74.9 us
    reduce_scatter x1, waiting for transfers between devices, reduce_mlp(): lax.psum_scatter(grad_down, ('fsdp', 'ctx'), scatter_dimension=0, tiled=T...  49.3 us
    psum x1, blocking collectives, local(): lax.psum((gain_one, gain_two, gain_q, gain_k), ('fsdp', 'ctx'))  41.8 us
  transfers between devices with their start and end apart: 15, of which 11 were waited for; matrix products, arithmetic and copies ran while one was open for 9% of the time, Pallas kernels for 0%

profile of v1, /device:TPU:11, one launch (start us, length us, event | category | flops | bytes accessed | tf_op | source)
XLA Modules:
  0.0 1648.8 jit_solution(7627294572984580907)
XLA Ops:
  7.3 1.8 convert_element_type.83
  10.0 1.2 fusion.66
  15.3 74.9 %all-gather.6.cloned.1.call-done = bf16[1024,4096]{1,0:T(8,128)(2,1)} async-done(((bf16[32,4096]{1,0:T(8,128)(2,1)}), bf16[1024,4096]{1,0:T(8,128)(2,1)}) %all-gather.6.cloned.1.call-update) | async-done | bytes 8388624 | tf_op jit(solution)/shard_map/all_gather | solution.py:158
  90.3 4.7 fusion.61
  104.0 14.7 collective-permute-done
  119.6 2.5 collective-permute-start.1
  123.0 1.2 collective-permute-done.1
  124.2 1.3 broadcast_select_fusion.7
  125.8 38.5 %collective-permute-done.2 = bf16[4,32,6144]{2,1,0:T(8,128)(2,1)} collective-permute-done((bf16[4,32,6144]{2,1,0:T(8,128)(2,1)S(1)}, bf16[4,32,6144]{2,1,0:T(8,128)(2,1)}, u32[]{:S(2)}, u32[]{:S(2)}) %collective-permute-start.2) | collective-permute-done | bytes 1572896 | tf_op jit(solution)/shard_map/ppermute | solution.py:37
  164.3 1.6 broadcast_select_fusion.5
  168.0 96.6 %collective-permute-done.3 = bf16[8,32,6144]{2,1,0:T(8,128)(2,1)} collective-permute-done((bf16[8,32,6144]{2,1,0:T(8,128)(2,1)S(1)}, bf16[8,32,6144]{2,1,0:T(8,128)(2,1)}, u32[]{:S(2)}, u32[]{:S(2)}) %collective-permute-start.3) | collective-permute-done | bytes 3145760 | tf_op jit(solution)/shard_map/ppermute | solution.py:37
  264.6 3.0 broadcast_select_fusion.3
  267.7 3.4 pad_maximum_fusion.1
  272.4 1.4 compare_and_fusion
  273.8 279.0 %collective-permute-done.4 = bf16[16,32,6144]{2,1,0:T(8,128)(2,1)} collective-permute-done((bf16[16,32,6144]{2,1,0:T(8,128)(2,1)}, bf16[16,32,6144]{2,1,0:T(8,128)(2,1)}, u32[]{:S(2)}, u32[]{:S(2)}) %collective-permute-start.4) | collective-permute-done | bytes 6291488 | tf_op jit(solution)/shard_map/ppermute | solution.py:37
  552.9 4.5 broadcast_select_fusion.1
  557.3 5.8 pad_maximum_fusion
  563.1 1.2 slice-done
  566.8 1.4 fusion.38
  568.3 1.1 copy.170
  569.5 1.9 fusion.88
  572.4 1.3 convolution_convert_fusion.1
  573.7 3.2 multiply_reduce_fusion.5
  578.0 8.1 fusion.77
  586.1 9.3 multiply_convert_fusion.1
  595.4 33.0 %all-gather.14.cloned.1.call-done = bf16[1024,6144]{1,0:T(8,128)(2,1)} async-done(((bf16[32,6144]{1,0:T(8,128)(2,1)}), bf16[1024,6144]{1,0:T(8,128)(2,1)}) %all-gather.14.cloned.1.call-update) | async-done | bytes 12582928 | tf_op jit(solution)/shard_map/all_gather | solution.py:228
  628.4 10.4 multiply_reduce_fusion.2
  639.7 2.3 convolution_convert_fusion
  642.0 2.1 copy.188
  644.1 3.2 fusion.48
  647.3 1.3 fusion.53
  648.6 4.1 fusion.6
  652.7 2.0 copy.186
  654.7 2.0 copy.187
  656.9 1.3 maximum_dynamic-update-slice_fusion
  658.3 1.1 slice.129
  659.5 7.6 fusion.89
  667.1 5.7 fusion.57
  672.9 13.4 fusion.24
  687.6 2.6 copy.151
  690.2 1.3 broadcast_bitcast_fusion
  692.6 2.6 copy.153
  695.2 1.4 copy.154
  696.6 1.4 copy.161
  698.0 4.6 fusion.7
  702.7 1.4 bitcast_multiply_fusion.9
  704.8 1.3 copy.152
  706.1 1.3 copy.185
  709.2 3.7 multiply_reduce_fusion
  712.9 1.9 convert_bitcast_fusion
  717.5 1.3 broadcast_multiply_fusion.1
  720.1 1.9 fusion.46
  722.7 8.9 fusion.50
  732.9 4.6 fusion.9
  737.7 6.5 fusion.37
  744.1 41.8 %all-reduce.1 = (f32[1024]{0:T(1024)S(1)}, f32[1024]{0:T(1024)S(1)}, f32[128]{0:T(128)S(1)}, f32[128]{0:T(128)S(1)}) all-reduce(f32[1024]{0:T(1024)S(1)} %get-tuple-element.36, f32[1024]{0:T(1024)S(1)} %copy-done.60, f32[128]{0:T(128)S(1)} %bitcast_reduce_fusion, ...), channel_id=1, replica_groups=mesh['fsdp'=16,'ctx'=2] {'fsdp','ctx'}, use_global_device_ids=true, to_apply=%region_21.22 | all-reduce | flops 2304 | bytes 18432 | tf_op jit(solution)/shard_map/psum | solution.py:299
  789.4 49.3 %reduce-scatter.14.cloned.1.call-done = f32[96,1024]{1,0:T(8,128)} async-done(((f32[3072,1024]{1,0:T(8,128)}), f32[96,1024]{1,0:T(8,128)}) %reduce-scatter.14.cloned.1.call-update) | async-done | bytes 393232 | tf_op jit(solution)/shard_map/reduce_scatter | solution.py:96
  838.7 2.4 multiply_subtract_fusion.2
  841.1 186.6 %reduce-scatter.10.cloned.1.call-done = f32[64,1024]{1,0:T(8,128)} async-done(((f32[2048,1024]{1,0:T(8,128)}), f32[64,1024]{1,0:T(8,128)}) %reduce-scatter.10.cloned.1.call-update) | async-done | bytes 262160 | tf_op jit(solution)/shard_map/reduce_scatter | solution.py:103
  1027.8 2.0 multiply_subtract_fusion.3
  1029.8 246.9 %reduce-scatter.12.cloned.1.call-done = f32[32,6144]{1,0:T(8,128)} async-done(((f32[1024,6144]{1,0:T(8,128)}), f32[32,6144]{1,0:T(8,128)}) %reduce-scatter.12.cloned.1.call-update) | async-done | bytes 786448 | tf_op jit(solution)/shard_map/reduce_scatter | solution.py:95
  1276.7 2.9 multiply_subtract_fusion
  1279.6 359.6 %reduce-scatter.8.cloned.1.call-done = f32[32,4096]{1,0:T(8,128)} async-done(((f32[1024,4096]{1,0:T(8,128)}), f32[32,4096]{1,0:T(8,128)}) %reduce-scatter.8.cloned.1.call-update) | async-done | bytes 524304 | tf_op jit(solution)/shard_map/reduce_scatter | solution.py:102
  1639.2 2.6 multiply_subtract_fusion.1
  (272 shorter events, 39.4 us)
Async XLA Ops:
  7.2 83.0 %copy-start.16 = (bf16[128,1024]{1,0:T(8,128)(2,1)S(1)}, bf16[128,1024]{1,0:T(8,128)(2,1)}, u32[]{:S(2)}) copy-start(bf16[128,1024]{1,0:T(8,128)(2,1)} %param.27) | copy-start | bytes 786436
  7.2 83.0 %all-gather.6.cloned.1.call-start = ((), (), s32[]{:S(2)}) async-start(), calls=%async_computation.5 | async-start | bytes 8650752 | tf_op jit(solution)/shard_map/all_gather | solution.py:158
  9.1 557.7 %all-gather.8.cloned.1.call-start = ((), (), s32[]{:S(2)}) async-start(), calls=%async_computation.6 | async-start | bytes 1572864 | tf_op jit(solution)/shard_map/all_gather | solution.py:185
  10.0 80.3 %copy-start.74 = (s32[4,1]{0,1:T(1,128)}, s32[4,1]{0,1:T(1,128)S(1)}, u32[]{:S(2)}) copy-start(s32[4,1]{0,1:T(1,128)S(1)} %reduce-window.8) | copy-start | bytes 52
  14.6 80.3 %copy-start.58 = (f32[128]{0:T(128)}, f32[128]{0:T(128)S(1)}, u32[]{:S(2)}) copy-start(f32[128]{0:T(128)S(1)} %get-tuple-element.108) | copy-start | bytes 1540
  95.0 5.3 copy-start.4
  96.0 4.0 copy-start.12
  100.3 3.3 copy-start.9
  102.0 471.7 %all-gather.10.cloned.1.call-start = ((), (), s32[]{:S(2)}) async-start(), calls=%async_computation.7 | async-start | bytes 4325376 | tf_op jit(solution)/shard_map/all_gather | solution.py:161
  102.7 483.4 %all-gather.12.cloned.1.call-start = ((), (), s32[]{:S(2)}) async-start(), calls=%async_computation.8 | async-start | bytes 6488064 | tf_op jit(solution)/shard_map/all_gather | solution.py:165
  103.5 524.8 %all-gather.14.cloned.1.call-start = ((), (), s32[]{:S(2)}) async-start(), calls=%async_computation.9 | async-start | bytes 12976128 | tf_op jit(solution)/shard_map/all_gather | solution.py:228
  103.6 15.1 collective-permute-start
  119.6 4.6 collective-permute-start.1
  123.0 589.9 %reduce-scatter.6.cloned.1.call-start = ((), (), s32[]{:S(2)}) async-start(), calls=%async_computation.10 | async-start | bytes 1572864 | tf_op jit(solution)/shard_map/reduce_scatter | solution.py:275
  125.7 38.6 %collective-permute-start.2 = (bf16[4,32,6144]{2,1,0:T(8,128)(2,1)S(1)}, bf16[4,32,6144]{2,1,0:T(8,128)(2,1)}, u32[]{:S(2)}, u32[]{:S(2)}) collective-permute-start(bf16[4,32,6144]{2,1,0:T(8,128)(2,1)S(1)} %pad_maximum_fusion.3), channel_id=1, source_target_pairs={{0,4},{1,5},{2,6},{3,7},{4,0},{5,1},{6,2},{7,3},{8,12},{9,13},{10,... | collective-permute-start | bytes 4718600 | tf_op jit(solution)/shard_map/ppermute | solution.py:37
  167.6 97.1 %collective-permute-start.3 = (bf16[8,32,6144]{2,1,0:T(8,128)(2,1)S(1)}, bf16[8,32,6144]{2,1,0:T(8,128)(2,1)}, u32[]{:S(2)}, u32[]{:S(2)}) collective-permute-start(bf16[8,32,6144]{2,1,0:T(8,128)(2,1)S(1)} %pad_maximum_fusion.2), channel_id=1, source_target_pairs={{0,8},{1,9},{2,10},{3,11},{4,12},{5,13},{6,14},{7,15},{8,0},{9,1},... | collective-permute-start | bytes 9437192 | tf_op jit(solution)/shard_map/ppermute | solution.py:37
  267.7 3.6 copy-start
  267.7 4.6 copy-start.75
  271.3 281.6 %collective-permute-start.4 = (bf16[16,32,6144]{2,1,0:T(8,128)(2,1)}, bf16[16,32,6144]{2,1,0:T(8,128)(2,1)}, u32[]{:S(2)}, u32[]{:S(2)}) collective-permute-start(bf16[16,32,6144]{2,1,0:T(8,128)(2,1)} %pad_maximum_fusion.1), channel_id=1, source_target_pairs={{0,16},{1,17},{2,18},{3,19},{4,20},{5,21},{6,22},{7,23},{8,24},{9,... | collective-permute-start | bytes 18874376 | tf_op jit(solution)/shard_map/ppermute | solution.py:37
  573.7 4.3 copy-start.42
  628.4 10.4 copy-start.2
  628.4 10.4 copy-start.36
  628.4 10.4 copy-start.57
  628.4 10.4 copy-start.83
  628.4 11.4 copy-start.6
  644.1 3.2 copy-start.22
  644.1 3.2 copy-start.53
  659.4 179.3 %reduce-scatter.14.cloned.1.call-start = ((), (), s32[]{:S(2)}) async-start(), calls=%async_computation.14 | async-start | bytes 12976128 | tf_op jit(solution)/shard_map/reduce_scatter | solution.py:96
  667.0 360.7 %reduce-scatter.10.cloned.1.call-start = ((), (), s32[]{:S(2)}) async-start(), calls=%async_computation.12 | async-start | bytes 8650752 | tf_op jit(solution)/shard_map/reduce_scatter | solution.py:103
  672.8 603.8 %reduce-scatter.12.cloned.1.call-start = ((), (), s32[]{:S(2)}) async-start(), calls=%async_computation.13 | async-start | bytes 25952256 | tf_op jit(solution)/shard_map/reduce_scatter | solution.py:95
  686.3 952.8 %reduce-scatter.8.cloned.1.call-start = ((), (), s32[]{:S(2)}) async-start(), calls=%async_computation.11 | async-start | bytes 17301504 | tf_op jit(solution)/shard_map/reduce_scatter | solution.py:102
  692.6 5.5 copy-start.54
  715.7 4.2 copy-start.50
  715.7 4.4 copy-start.18
  715.7 4.4 copy-start.20
  719.8 2.8 copy-start.28
  732.9 4.6 copy-start.29
  732.9 4.6 copy-start.33
  732.9 4.6 copy-start.35
  737.5 6.6 copy-start.60
  737.5 48.5 %copy-start.66 = (f32[128]{0:T(128)S(1)}, f32[128]{0:T(128)}, u32[]{:S(2)}) copy-start(f32[128]{0:T(128)} %param.51) | copy-start | bytes 1540
  737.5 48.5 %copy-start.76 = (f32[128]{0:T(128)S(1)}, f32[128]{0:T(128)}, u32[]{:S(2)}) copy-start(f32[128]{0:T(128)} %param.52) | copy-start | bytes 1540
  737.5 48.5 %copy-start.77 = (f32[128]{0:T(128)S(1)}, f32[128]{0:T(128)}, u32[]{:S(2)}) copy-start(f32[128]{0:T(128)} %param.53) | copy-start | bytes 1540
  737.6 49.0 %copy-start.63 = (f32[128]{0:T(128)S(1)}, f32[128]{0:T(128)}, u32[]{:S(2)}) copy-start(f32[128]{0:T(128)} %param.48) | copy-start | bytes 1540
  737.6 49.0 %copy-start.78 = (f32[128]{0:T(128)S(1)}, f32[128]{0:T(128)}, u32[]{:S(2)}) copy-start(f32[128]{0:T(128)} %param.49) | copy-start | bytes 1540
  737.6 49.0 %copy-start.79 = (f32[128]{0:T(128)S(1)}, f32[128]{0:T(128)}, u32[]{:S(2)}) copy-start(f32[128]{0:T(128)} %param.50) | copy-start | bytes 1540
  737.6 49.5 %copy-start.67 = (f32[1024]{0:T(1024)S(1)}, f32[1024]{0:T(1024)}, u32[]{:S(2)}) copy-start(f32[1024]{0:T(1024)} %param.46) | copy-start | bytes 12292
  737.6 49.5 %copy-start.68 = (f32[1024]{0:T(1024)S(1)}, f32[1024]{0:T(1024)}, u32[]{:S(2)}) copy-start(f32[1024]{0:T(1024)} %param.47) | copy-start | bytes 12292
  737.6 50.1 %copy-start.69 = (f32[1024]{0:T(1024)S(1)}, f32[1024]{0:T(1024)}, u32[]{:S(2)}) copy-start(f32[1024]{0:T(1024)} %param.43) | copy-start | bytes 12292
  737.6 50.1 %copy-start.70 = (f32[1024]{0:T(1024)S(1)}, f32[1024]{0:T(1024)}, u32[]{:S(2)}) copy-start(f32[1024]{0:T(1024)} %param.44) | copy-start | bytes 12292
  737.6 50.7 %copy-start.15 = (f32[128,1024]{1,0:T(8,128)S(1)}, f32[128,1024]{1,0:T(8,128)}, u32[]{:S(2)}) copy-start(f32[128,1024]{1,0:T(8,128)} %copy-done.14) | copy-start | bytes 1572868
  737.7 50.7 %copy-start.82 = (f32[128]{0:T(128)S(1)}, f32[128]{0:T(128)}, u32[]{:S(2)}) copy-start(f32[128]{0:T(128)} %get-tuple-element.107) | copy-start | bytes 1540
  744.1 94.6 %copy-start.31 = (f32[96,1024]{1,0:T(8,128)S(1)}, f32[96,1024]{1,0:T(8,128)}, u32[]{:S(2)}) copy-start(f32[96,1024]{1,0:T(8,128)} %param.39) | copy-start | bytes 1179652
  786.0 55.1 %copy-start.71 = (f32[1024]{0:T(1024)}, f32[1024]{0:T(1024)S(1)}, u32[]{:S(2)}) copy-start(f32[1024]{0:T(1024)S(1)} %get-tuple-element.40) | copy-start | bytes 12292
  786.0 55.1 %copy-start.72 = (f32[1024]{0:T(1024)}, f32[1024]{0:T(1024)S(1)}, u32[]{:S(2)}) copy-start(f32[1024]{0:T(1024)S(1)} %get-tuple-element.41) | copy-start | bytes 12292
  786.0 55.1 %copy-start.80 = (f32[128]{0:T(128)}, f32[128]{0:T(128)S(1)}, u32[]{:S(2)}) copy-start(f32[128]{0:T(128)S(1)} %get-tuple-element.42) | copy-start | bytes 1540
  786.0 55.1 %copy-start.81 = (f32[128]{0:T(128)}, f32[128]{0:T(128)S(1)}, u32[]{:S(2)}) copy-start(f32[128]{0:T(128)S(1)} %get-tuple-element.43) | copy-start | bytes 1540
  788.4 239.4 %copy-start.38 = (f32[64,1024]{1,0:T(8,128)S(1)}, f32[64,1024]{1,0:T(8,128)}, u32[]{:S(2)}) copy-start(f32[64,1024]{1,0:T(8,128)} %param.33) | copy-start | bytes 786436
  789.4 238.4 %copy-start.49 = (f32[64,1024]{1,0:T(8,128)S(1)}, f32[64,1024]{1,0:T(8,128)}, u32[]{:S(2)}) copy-start(f32[64,1024]{1,0:T(8,128)} %param.34) | copy-start | bytes 786436
  789.4 487.3 %copy-start.10 = (f32[32,6144]{1,0:T(8,128)S(1)}, f32[32,6144]{1,0:T(8,128)}, u32[]{:S(2)}) copy-start(f32[32,6144]{1,0:T(8,128)} %param.36) | copy-start | bytes 2359300
  789.4 487.3 %copy-start.40 = (f32[32,6144]{1,0:T(8,128)S(1)}, f32[32,6144]{1,0:T(8,128)}, u32[]{:S(2)}) copy-start(f32[32,6144]{1,0:T(8,128)} %param.37) | copy-start | bytes 2359300
  789.4 487.3 %copy-start.41 = (f32[32,6144]{1,0:T(8,128)S(1)}, f32[32,6144]{1,0:T(8,128)}, u32[]{:S(2)}) copy-start(f32[32,6144]{1,0:T(8,128)} %param.38) | copy-start | bytes 2359300
  1029.8 609.4 %copy-start.27 = (f32[32,4096]{1,0:T(8,128)S(1)}, f32[32,4096]{1,0:T(8,128)}, u32[]{:S(2)}) copy-start(f32[32,4096]{1,0:T(8,128)} %param.30) | copy-start | bytes 1572868
  1029.8 609.4 %copy-start.48 = (f32[32,4096]{1,0:T(8,128)S(1)}, f32[32,4096]{1,0:T(8,128)}, u32[]{:S(2)}) copy-start(f32[32,4096]{1,0:T(8,128)} %param.31) | copy-start | bytes 1572868
  (36 other events, 52.6 us)
Sparse Core Ops, SparseCore 0:
  11.6 78.6 all-gather.5
  102.1 24.0 all-gather.7
  129.7 70.0 all-gather.9
  203.2 78.5 all-gather.11
  285.1 343.1 all-gather.13
  659.5 17.7 reduce-scatter.5
  683.9 154.7 reduce-scatter.13
  841.5 186.1 reduce-scatter.9
  1034.8 241.8 reduce-scatter.11
  1279.4 359.7 reduce-scatter.7
